TPU v7x, 32 devices: a whole 2x2x4 slice. The times are simulated.
32 devices in a mesh: rep: 16 (over z, y, core), fsdp: 2 (over x).
Axes of the slice: x: 2, y: 2, z: 4, core: 2. Of those that a mesh axis runs over, the one named last changes fastest.
Arguments:
- activations: bfloat16 [4096, 8192], P(('rep', 'fsdp')), may hold values from -7.75 to 7.75
- upstream: bfloat16 [4096, 512], P(('rep', 'fsdp')), may hold values from -0.484375 to 0.484375
- q_start: float32 [2, 4, 512], P('fsdp'), may hold values from -6 to 6
Outputs:
- error_feedback: bfloat16 [16, 8192, 512], P('rep', 'fsdp')
- p_basis: float32 [2, 4, 4096], P('fsdp')
- q_factor: float32 [2, 4, 512], P('fsdp')
All inputs are finite; a program needn't handle non-finite values.
Results may differ from a plain program's by a relative error of at most 0.015.
Values may be sent and summed in bfloat16 or wider, within the bound.
A program may use at most 64 MiB of HBM per device.

v0:
```python
import jax
import jax.numpy as jnp
from jax import lax
from jax.sharding import PartitionSpec as P


def contract_tokens(left, right):
    return lax.dot_general(
        left, right, (((0,), (0,)), ((), ())), preferred_element_type=jnp.float32
    )


def rounded(term):
    short = lax.optimization_barrier(term.astype(jnp.bfloat16))
    return short.astype(jnp.float32)


def on_device(activations, upstream, q_start):
    high = lax.Precision.HIGHEST
    groups = lax.axis_size("fsdp")
    replicas = lax.axis_size("rep")
    tok_rows = activations.shape[0]
    shard_rows = activations.shape[1] // groups
    columns = lax.all_to_all(activations, "fsdp", split_axis=1, concat_axis=0, tiled=True)
    cotangent_all = lax.all_gather(upstream, "fsdp", axis=0, tiled=True)
    shard = jnp.zeros((shard_rows, upstream.shape[1]), jnp.float32)
    for source in range(groups):
        left = columns[source * tok_rows : (source + 1) * tok_rows]
        right = cotangent_all[source * tok_rows : (source + 1) * tok_rows]
        shard = shard + rounded(contract_tokens(left, right))
    q_local = q_start[0]
    left_local = lax.dot_general(
        q_local, shard, (((1,), (1,)), ((), ())), precision=high, preferred_element_type=jnp.float32
    )
    p_sum = lax.psum(left_local, "rep")
    basis = []
    for i in range(p_sum.shape[0]):
        vector = p_sum[i]
        for earlier in basis:
            vector = vector - jnp.sum(vector * earlier) * earlier
        basis.append(vector / jnp.sqrt(jnp.sum(vector * vector) + 1e-06))
    p_basis = jnp.stack(basis)
    right_local = jnp.dot(p_basis, shard, precision=high)
    q_factor = lax.psum(right_local, "rep")
    approx = lax.dot_general(
        p_basis,
        q_factor / replicas,
        (((0,), (0,)), ((), ())),
        precision=high,
        preferred_element_type=jnp.float32,
    )
    error_feedback = (shard - approx).astype(jnp.bfloat16)
    return (error_feedback[None], p_basis[None], q_factor[None])


def solution(mesh):
    in_specs = (P(("rep", "fsdp"), None), P(("rep", "fsdp"), None), P("fsdp", None, None))
    out_specs = (P("rep", "fsdp", None), P("fsdp", None, None), P("fsdp", None, None))
    return jax.shard_map(
        on_device, mesh=mesh, in_specs=in_specs, out_specs=out_specs, check_vma=False
    )
```

profile of v0, /device:TPU:0, one launch (start us, length us, event | category | flops | bytes accessed | tf_op | source)
XLA Modules:
  0.0 222.7 jit_solution(16569028851342070702)
XLA Ops:
  7.2 0.0 copy-start
  7.2 0.0 copy-start.3
  7.2 4.1 %copy.6 = bf16[128,8192]{0,1:T(8,128)(2,1)} copy(bf16[128,8192]{1,0:T(8,128)(2,1)} %param.3) | data formatting | bytes 4194304 | tf_op args[0]
  11.3 4.2 %all-to-all-start = ((bf16[128,2,4096]{0,2,1:T(8,128)(2,1)}), bf16[128,2,4096]{0,2,1:T(8,128)(2,1)S(1)}, u32[]{:S(2)}, u32[]{:S(2)}) async-start(bf16[128,2,4096]{0,2,1:T(8,128)(2,1)} %bitcast.26), calls=%async_computation | async-start | bytes 4194304 | tf_op jit(solution)/shard_map/all_to_all | solution.py:24
  15.5 0.0 all-reduce.2.cloned.1.call-start
  15.5 0.0 copy-done.3
  15.5 28.7 %all_gather.3 = bf16[256,512]{1,0:T(8,128)(2,1)S(1)} all-gather(bf16[128,512]{1,0:T(8,128)(2,1)S(1)} %copy-done.3), channel_id=1, replica_groups=mesh['rep'=16,'fsdp'=2] {'fsdp'}, dimensions={0}, use_global_device_ids=true | all-gather | bytes 393216 | tf_op jit(solution)/shard_map/all_gather | solution.py:25
  44.2 0.0 all-to-all-done
  44.2 1.2 convolution_convert_fusion
  45.4 0.0 copy-start.1
  45.5 1.2 convolution_convert_fusion.1
  46.7 0.8 copy-done.1
  47.5 0.0 copy-start.2
  47.5 1.9 copy-done.2
  49.4 0.0 copy-done
  49.4 8.4 %fusion.3 = f32[4,4096]{1,0:T(4,128)} fusion(bf16[4096,512]{1,0:T(8,128)(2,1)S(1)} %convolution_convert_fusion, bf16[4096,512]{1,0:T(8,128)(2,1)S(1)} %convolution_convert_fusion.1, f32[1,4,512]{2,1,0:T(4,128)S(1)} %copy-done), kind=kOutput, calls=%fused_computation.7 | convolution fusion | flops 106954752 | bytes 8462336 | tf_op jit(solution)/shard_map/dot_general | solution.py:32
  57.8 0.0 all-reduce.2.cloned.1.call-update
  57.9 87.0 %all-reduce.2.cloned.1.call-done = f32[4,4096]{1,0:T(4,128)} async-done(((f32[4,4096]{1,0:T(4,128)}), f32[4,4096]{1,0:T(4,128)}) %all-reduce.2.cloned.1.call-update) | async-done | bytes 65552 | tf_op jit(solution)/shard_map/psum | solution.py:35
  144.8 1.5 multiply_reduce_fusion.9
  147.0 1.1 fusion.11
  148.1 0.6 multiply_reduce_fusion.8
  148.7 1.3 multiply_reduce_fusion.3
  150.7 2.5 %multiply_reduce_fusion.2 = (f32[]{:T(128)}, f32[]{:T(128)}, f32[4096]{0:T(1024)S(1)}) fusion(f32[4096]{0:T(1024)S(1)} %bitcast.36, f32[4096]{0:T(1024)S(1)} %bitcast.29, f32[]{:T(128)} %get-tuple-element.5, f32[4096]{0:T(1024)S(1)} %bitcast.39, f32[]{:T(128)} %get-tuple-element.6, f32[]{:T(128)S(6)} %sqrt.13, f32[4096]{0:T(1024)S(1)} %bitcast.34, ...), kind=kLoop, calls=%fused_computation.17 | loop fusion | flops 45054 | bytes 81944 | tf_op jit(solution)/shard_map/reduce_sum | solution.py:40
  153.2 1.8 multiply_reduce_fusion.4
  155.7 1.9 multiply_reduce_fusion.1
  157.6 1.3 multiply_reduce_fusion
  159.5 4.8 %subtract_divide_fusion = (f32[1,4096]{1,0:T(1,128)S(1)}, f32[1,4096]{1,0:T(1,128)S(1)}, f32[1,4096]{1,0:T(1,128)S(1)}) fusion(f32[1,4096]{1,0:T(1,128)S(1)} %get-tuple-element.17, f32[]{:T(128)S(6)} %sqrt.15, f32[]{:T(128)} %get-tuple-element.11, f32[]{:T(128)} %get-tuple-element.3, f32[]{:T(128)} %get-tuple-element.5, ...), kind=kLoop, calls=%fused_computation.14 | loop fusion | flops 61440 | bytes 114724 | tf_op jit(solution)/shard_map/div | solution.py:41
  164.3 7.1 %fusion = f32[4,512]{1,0:T(4,128)S(1)} fusion(bf16[4096,512]{1,0:T(8,128)(2,1)} %copy-done.1, bf16[4096,512]{1,0:T(8,128)(2,1)} %copy-done.2, f32[1,4096]{1,0:T(1,128)S(1)} %get-tuple-element.8, f32[1,4096]{1,0:T(1,128)S(1)} %get-tuple-element.9, f32[1,4096]{1,0:T(1,128)S(1)} %get-tuple-element.10, f32[1,4096]{1,0:T(1,128)S(1)} %get-tuple-element.17), kind=kOutput, calls=%fused_computation.2 | convolution fusion | flops 107003904 | bytes 8462336 | tf_op jit(solution)/shard_map/dot_general | solution.py:43
  171.4 0.7 fusion.10
  172.1 32.4 %psum.15 = f32[4,512]{1,0:T(4,128)S(1)} all-reduce(f32[4,512]{1,0:T(4,128)S(1)} %fusion), channel_id=1, replica_groups=mesh['rep'=16,'fsdp'=2] {'rep'}, use_global_device_ids=true, to_apply=%region_11.0 | all-reduce | flops 2048 | bytes 16384 | tf_op jit(solution)/shard_map/psum | solution.py:44
  204.6 0.0 copy-start.4
  204.6 11.3 %fusion.2 = bf16[1,4096,512]{2,1,0:T(8,128)(2,1)} fusion(bf16[4096,512]{1,0:T(8,128)(2,1)} %copy-done.1, bf16[4096,512]{1,0:T(8,128)(2,1)} %copy-done.2, f32[4,512]{1,0:T(4,128)S(1)} %psum.15, f32[1,4096]{1,0:T(1,128)S(1)} %get-tuple-element.8, f32[1,4096]{1,0:T(1,128)S(1)} %get-tuple-element.9, f32[1,4096]{1,0:T(1,128)S(1)} %get-tuple-element.10, ...), kind=kOutput, calls=%fused_computation.6 | convolution fusion | flops 111200256 | bytes 12656640 | tf_op jit(solution)/shard_map/dot_general | solution.py:45
  215.9 0.0 copy-done.4
Async XLA Ops:
  7.2 42.2 %copy-start = (f32[1,4,512]{2,1,0:T(4,128)S(1)}, f32[1,4,512]{2,1,0:T(4,128)}, u32[]{:S(2)}) copy-start(f32[1,4,512]{2,1,0:T(4,128)} %param.5) | copy-start | bytes 24580
  7.2 8.4 %copy-start.3 = (bf16[128,512]{1,0:T(8,128)(2,1)S(1)}, bf16[128,512]{1,0:T(8,128)(2,1)}, u32[]{:S(2)}) copy-start(bf16[128,512]{1,0:T(8,128)(2,1)} %param.4) | copy-start | bytes 393220
  11.3 32.9 %all-to-all-start = ((bf16[128,2,4096]{0,2,1:T(8,128)(2,1)}), bf16[128,2,4096]{0,2,1:T(8,128)(2,1)S(1)}, u32[]{:S(2)}, u32[]{:S(2)}) async-start(bf16[128,2,4096]{0,2,1:T(8,128)(2,1)} %bitcast.26), calls=%async_computation | async-start | bytes 4194304 | tf_op jit(solution)/shard_map/all_to_all | solution.py:24
  15.5 129.3 %all-reduce.2.cloned.1.call-start = ((), (), s32[]{:S(2)}) async-start(), calls=%async_computation.1 | async-start | bytes 131072 | tf_op jit(solution)/shard_map/psum | solution.py:35
  45.4 2.0 copy-start.1
  47.5 1.9 copy-start.2
  204.6 11.3 %copy-start.4 = (f32[4,512]{1,0:T(4,128)}, f32[4,512]{1,0:T(4,128)S(1)}, u32[]{:S(2)}) copy-start(f32[4,512]{1,0:T(4,128)S(1)} %psum.15) | copy-start | bytes 24580
Sparse Core Ops, SparseCore 0:
  58.0 86.7 all-reduce.1
where the time goes:
time: 223 us
  waiting for transfers between devices  87 us (39%)
  blocking collectives  61.1 us (27%)
  matrix products  29.3 us (13%)
  other arithmetic  17.4 us (8%)
  between operations  16.8 us (8%)
  local copies, waits for them, and re-layouts  6.82 us (3%)
  starting transfers between devices  4.24 us (2%)
    psum x1, waiting for transfers between devices, on_device(): p_sum = lax.psum(left_local, 'rep')  87 us
    psum x1, blocking collectives, on_device(): q_factor = lax.psum(right_local, 'rep')  32.4 us
    all_gather x1, blocking collectives, on_device(): cotangent_all = lax.all_gather(upstream, 'fsdp', axis=0, tiled=True)  28.7 us
    dot_general x1, matrix products, on_device(): lax.dot_general(p_basis, q_factor / replicas, (((0,), (0,)), ((), ())), p...  11.3 us
    dot_general x1, matrix products, on_device(): lax.dot_general(q_local, shard, (((1,), (1,)), ((), ())), precision=high,...  8.44 us
    dot_general x1, matrix products, on_device(): right_local = jnp.dot(p_basis, shard, precision=high)  7.14 us
    unnamed x11, local copies, waits for them, and re-layouts  6.82 us
    reduce_sum x4, other arithmetic, on_device(): vector = vector - jnp.sum(vector * earlier) * earlier  6.39 us
  transfers between devices with their start and end apart: 2, of which 1 were waited for; matrix products, arithmetic and copies ran while one was open for 0% of the time, Pallas kernels for 0%

commit v1 on v0

--- a/solution.py
+++ b/solution.py
@@ -41,7 +41,7 @@
         basis.append(vector / jnp.sqrt(jnp.sum(vector * vector) + 1e-06))
     p_basis = jnp.stack(basis)
     right_local = jnp.dot(p_basis, shard, precision=high)
-    q_factor = lax.psum(right_local, "rep")
+    q_factor = jnp.sum(lax.all_gather(right_local, "rep"), axis=0)
     approx = lax.dot_general(
         p_basis,
         q_factor / replicas,

time: 223 us -> 213 us (0.955)
  blocking collectives: 61.1 us -> 51.1 us
    psum x1 -> x0, blocking collectives: 32.4 us -> none  [on_device(): q_factor = lax.psum(right_local, 'rep')]
    all_gather x0 -> x1, blocking collectives: none -> 22.4 us  [on_device(): q_factor = jnp.sum(lax.all_gather(right_local, 'rep'), axis=0)]
where the time goes in v1:
time: 213 us
  waiting for transfers between devices  87 us (41%)
  blocking collectives  51.1 us (24%)
  matrix products  29.3 us (14%)
  other arithmetic  17.5 us (8%)
  between operations  16.8 us (8%)
  local copies, waits for them, and re-layouts  6.81 us (3%)
  starting transfers between devices  4.24 us (2%)
    psum x1, waiting for transfers between devices, on_device(): p_sum = lax.psum(left_local, 'rep')  87 us
    all_gather x1, blocking collectives, on_device(): cotangent_all = lax.all_gather(upstream, 'fsdp', axis=0, tiled=True)  28.7 us
    all_gather x1, blocking collectives, on_device(): q_factor = jnp.sum(lax.all_gather(right_local, 'rep'), axis=0)  22.4 us
    dot_general x1, matrix products, on_device(): lax.dot_general(p_basis, q_factor / replicas, (((0,), (0,)), ((), ())), p...  11.3 us
    dot_general x1, matrix products, on_device(): lax.dot_general(q_local, shard, (((1,), (1,)), ((), ())), precision=high,...  8.44 us
    dot_general x1, matrix products, on_device(): right_local = jnp.dot(p_basis, shard, precision=high)  7.14 us
    unnamed x11, local copies, waits for them, and re-layouts  6.81 us
    reduce_sum x4, other arithmetic, on_device(): vector = vector - jnp.sum(vector * earlier) * earlier  6.39 us
  transfers between devices with their start and end apart: 2, of which 1 were waited for; matrix products, arithmetic and copies ran while one was open for 0% of the time, Pallas kernels for 0%

profile of v1, /device:TPU:0, one launch (start us, length us, event | category | flops | bytes accessed | tf_op | source)
XLA Modules:
  0.0 212.8 jit_solution(2980421579178745298)
XLA Ops:
  7.2 0.0 copy-start
  7.2 0.0 copy-start.3
  7.2 4.1 %copy.9 = bf16[128,8192]{0,1:T(8,128)(2,1)} copy(bf16[128,8192]{1,0:T(8,128)(2,1)} %param.3) | data formatting | bytes 4194304 | tf_op args[0]
  11.3 4.2 %all-to-all-start = ((bf16[128,2,4096]{0,2,1:T(8,128)(2,1)}), bf16[128,2,4096]{0,2,1:T(8,128)(2,1)S(1)}, u32[]{:S(2)}, u32[]{:S(2)}) async-start(bf16[128,2,4096]{0,2,1:T(8,128)(2,1)} %bitcast.28), calls=%async_computation | async-start | bytes 4194304 | tf_op jit(solution)/shard_map/all_to_all | solution.py:24
  15.5 0.0 all-reduce.2.cloned.1.call-start
  15.5 0.0 copy-done.3
  15.5 28.7 %all_gather.9 = bf16[256,512]{1,0:T(8,128)(2,1)S(1)} all-gather(bf16[128,512]{1,0:T(8,128)(2,1)S(1)} %copy-done.3), channel_id=1, replica_groups=mesh['rep'=16,'fsdp'=2] {'fsdp'}, dimensions={0}, use_global_device_ids=true | all-gather | bytes 393216 | tf_op jit(solution)/shard_map/all_gather | solution.py:25
  44.2 0.0 all-to-all-done
  44.2 1.2 convolution_convert_fusion
  45.4 0.0 copy-start.1
  45.5 1.2 convolution_convert_fusion.1
  46.7 0.8 copy-done.1
  47.5 0.0 copy-start.2
  47.5 1.9 copy-done.2
  49.4 0.0 copy-done
  49.4 8.4 %fusion.3 = f32[4,4096]{1,0:T(4,128)} fusion(bf16[4096,512]{1,0:T(8,128)(2,1)S(1)} %convolution_convert_fusion, bf16[4096,512]{1,0:T(8,128)(2,1)S(1)} %convolution_convert_fusion.1, f32[1,4,512]{2,1,0:T(4,128)S(1)} %copy-done), kind=kOutput, calls=%fused_computation.7 | convolution fusion | flops 106954752 | bytes 8462336 | tf_op jit(solution)/shard_map/dot_general | solution.py:32
  57.8 0.0 all-reduce.2.cloned.1.call-update
  57.9 87.0 %all-reduce.2.cloned.1.call-done = f32[4,4096]{1,0:T(4,128)} async-done(((f32[4,4096]{1,0:T(4,128)}), f32[4,4096]{1,0:T(4,128)}) %all-reduce.2.cloned.1.call-update) | async-done | bytes 65552 | tf_op jit(solution)/shard_map/psum | solution.py:35
  144.8 1.5 multiply_reduce_fusion.9
  147.0 1.1 fusion.12
  148.1 0.6 multiply_reduce_fusion.8
  148.7 1.3 multiply_reduce_fusion.3
  150.7 2.5 %multiply_reduce_fusion.2 = (f32[]{:T(128)}, f32[]{:T(128)}, f32[4096]{0:T(1024)S(1)}) fusion(f32[4096]{0:T(1024)S(1)} %bitcast.38, f32[4096]{0:T(1024)S(1)} %bitcast.31, f32[]{:T(128)} %get-tuple-element.5, f32[4096]{0:T(1024)S(1)} %bitcast.41, f32[]{:T(128)} %get-tuple-element.6, f32[]{:T(128)S(6)} %sqrt.13, f32[4096]{0:T(1024)S(1)} %bitcast.36, ...), kind=kLoop, calls=%fused_computation.18 | loop fusion | flops 45054 | bytes 81944 | tf_op jit(solution)/shard_map/reduce_sum | solution.py:40
  153.2 1.8 multiply_reduce_fusion.4
  155.7 1.9 multiply_reduce_fusion.1
  157.6 1.3 multiply_reduce_fusion
  159.5 4.8 %subtract_divide_fusion = (f32[1,4096]{1,0:T(1,128)S(1)}, f32[1,4096]{1,0:T(1,128)S(1)}, f32[1,4096]{1,0:T(1,128)S(1)}) fusion(f32[1,4096]{1,0:T(1,128)S(1)} %get-tuple-element.17, f32[]{:T(128)S(6)} %sqrt.15, f32[]{:T(128)} %get-tuple-element.11, f32[]{:T(128)} %get-tuple-element.3, f32[]{:T(128)} %get-tuple-element.5, ...), kind=kLoop, calls=%fused_computation.15 | loop fusion | flops 61440 | bytes 114724 | tf_op jit(solution)/shard_map/div | solution.py:41
  164.3 7.1 %fusion.4 = f32[1,4,512]{2,1,0:T(4,128)S(1)} fusion(bf16[4096,512]{1,0:T(8,128)(2,1)} %copy-done.1, bf16[4096,512]{1,0:T(8,128)(2,1)} %copy-done.2, f32[1,4096]{1,0:T(1,128)S(1)} %get-tuple-element.8, f32[1,4096]{1,0:T(1,128)S(1)} %get-tuple-element.9, f32[1,4096]{1,0:T(1,128)S(1)} %get-tuple-element.10, f32[1,4096]{1,0:T(1,128)S(1)} %get-tuple-element.17), kind=kOutput, calls=%fused_computation.8 | convolution fusion | flops 107003904 | bytes 8462336 | tf_op jit(solution)/shard_map/dot_general | solution.py:43
  171.4 0.7 fusion.11
  172.1 22.4 %all-gather.1 = f32[16,4,512]{2,1,0:T(4,128)S(1)} all-gather(f32[1,4,512]{2,1,0:T(4,128)S(1)} %fusion.4), channel_id=2, replica_groups=mesh['rep'=16,'fsdp'=2] {'rep'}, dimensions={0}, use_global_device_ids=true | all-gather | bytes 139264 | tf_op jit(solution)/shard_map/all_gather | solution.py:44
  194.6 0.0 copy-start.4
  194.6 11.3 %fusion.2 = bf16[1,4096,512]{2,1,0:T(8,128)(2,1)} fusion(bf16[4096,512]{1,0:T(8,128)(2,1)} %copy-done.1, bf16[4096,512]{1,0:T(8,128)(2,1)} %copy-done.2, f32[4,512]{1,0:T(4,128)S(1)} %reduce_sum.109, f32[1,4096]{1,0:T(1,128)S(1)} %get-tuple-element.8, f32[1,4096]{1,0:T(1,128)S(1)} %get-tuple-element.9, f32[1,4096]{1,0:T(1,128)S(1)} %get-tuple-element.10, ...), kind=kOutput, calls=%fused_computation.6 | convolution fusion | flops 111200256 | bytes 12656640 | tf_op jit(solution)/shard_map/dot_general | solution.py:45
  205.9 0.0 copy-done.4
  (1 shorter events, 0.0 us)
Async XLA Ops:
  7.2 42.2 %copy-start = (f32[1,4,512]{2,1,0:T(4,128)S(1)}, f32[1,4,512]{2,1,0:T(4,128)}, u32[]{:S(2)}) copy-start(f32[1,4,512]{2,1,0:T(4,128)} %param.5) | copy-start | bytes 24580
  7.2 8.4 %copy-start.3 = (bf16[128,512]{1,0:T(8,128)(2,1)S(1)}, bf16[128,512]{1,0:T(8,128)(2,1)}, u32[]{:S(2)}) copy-start(bf16[128,512]{1,0:T(8,128)(2,1)} %param.4) | copy-start | bytes 393220
  11.3 32.9 %all-to-all-start = ((bf16[128,2,4096]{0,2,1:T(8,128)(2,1)}), bf16[128,2,4096]{0,2,1:T(8,128)(2,1)S(1)}, u32[]{:S(2)}, u32[]{:S(2)}) async-start(bf16[128,2,4096]{0,2,1:T(8,128)(2,1)} %bitcast.28), calls=%async_computation | async-start | bytes 4194304 | tf_op jit(solution)/shard_map/all_to_all | solution.py:24
  15.5 129.3 %all-reduce.2.cloned.1.call-start = ((), (), s32[]{:S(2)}) async-start(), calls=%async_computation.1 | async-start | bytes 131072 | tf_op jit(solution)/shard_map/psum | solution.py:35
  45.4 2.0 copy-start.1
  47.5 1.9 copy-start.2
  194.6 11.3 %copy-start.4 = (f32[4,512]{1,0:T(4,128)}, f32[4,512]{1,0:T(4,128)S(1)}, u32[]{:S(2)}) copy-start(f32[4,512]{1,0:T(4,128)S(1)} %reduce_sum.109) | copy-start | bytes 24580
Sparse Core Ops, SparseCore 0:
  58.0 86.7 all-reduce.1
